TPU v7x, 32 devices: a whole 2x2x4 slice. The times are simulated.
32 devices in a mesh: row: 8 (over z, y), col: 4 (over x, core).
Axes of the slice: x: 2, y: 2, z: 4, core: 2. Of those that a mesh axis runs over, the one named last changes fastest.
Arguments:
- tensor: bfloat16 [1024, 64, 512], P('row', None, 'col'), may hold values from -6 to 6
- loss_kind: int32 [1024, 64, 512], P('row', None, 'col'), may hold values from 0 to 1, as said below
- factor_one: float32 [1024, 512], P(('row', 'col')), may hold values from -2 to 2
- factor_two: float32 [512, 512], P(('col', 'row')), may hold values from -2 to 2
- factor_three: float32 [64, 512], replicated, may hold values from -2 to 2
- first_one: float32 [1024, 512], P(('row', 'col')), may hold values from -0.03 to 0.03
- second_one: float32 [1024, 512], P(('row', 'col')), may hold values from 0.0005 to 0.05
- first_two: float32 [512, 512], P(('col', 'row')), may hold values from -0.03 to 0.03
- second_two: float32 [512, 512], P(('col', 'row')), may hold values from 0.0005 to 0.05
- first_three: float32 [64, 512], replicated, may hold values from -0.03 to 0.03
- second_three: float32 [64, 512], replicated, may hold values from 0.0005 to 0.05
Outputs:
- new_one: float32 [1024, 512], P(('row', 'col'))
- new_two: float32 [512, 512], P(('col', 'row'))
- new_three: float32 [64, 512], replicated
Inputs may be any that keep to these rules, and one draw needn't show every extreme that they name: loss_kind takes one value on each block of 128 first-mode by 128 second-mode indices (with all 64 third-mode ones), aligned to multiples of 128 and 128, and is 1 on exactly half of these blocks.
All inputs are finite; a program needn't handle non-finite values.
Results may differ from a plain program's by a relative error of at most 0.003.
Values may be sent and summed in bfloat16 or wider, within the bound.
A program may use at most 128 MiB of HBM per device.

v0:
```python
import math
import jax
import jax.numpy as jnp
from jax import lax
from jax.sharding import PartitionSpec as P

ITERS = 2
STEP = 10
learn_rate = 0.05
beta_one = 0.8
beta_two = 0.95
adam_eps = 1e-08


def loss_slope(rebuilt, values, kinds):
    excess = rebuilt - values
    huber_part = jnp.clip(excess, -1.0, 1.0)
    target = jnp.where(values > 0, 1.0, 0.0).astype(rebuilt.dtype)
    logit_part = jax.nn.sigmoid(rebuilt) - target
    return jnp.where(kinds == 1, logit_part, huber_part)


def adam_step(param, first, second, grad, counter):
    first = beta_one * first + (1.0 - beta_one) * grad
    second = beta_two * second + (1.0 - beta_two) * grad * grad
    corr_one = 1.0 - beta_one**counter
    corr_two = 1.0 - beta_two**counter
    param = param - learn_rate * (first / corr_one) / (jnp.sqrt(second / corr_two) + adam_eps)
    return (param, first, second)


def tile_grads(tensor, loss_kind, half_one, half_two, half_three, scales):
    tile_rows, tile_depth, tile_cols = tensor.shape
    rank_width = half_one.shape[1]
    one_f = half_one.astype(jnp.float32)
    three_f = half_three.astype(jnp.float32)
    scaled_rows = (
        (one_f[:, None, :] * three_f[None, :, :])
        .astype(jnp.bfloat16)
        .reshape(tile_rows * tile_depth, rank_width)
    )
    rebuilt = lax.dot_general(
        scaled_rows, half_two, (((1,), (1,)), ((), ())), preferred_element_type=jnp.float32
    )
    values = tensor.reshape(tile_rows * tile_depth, tile_cols).astype(jnp.float32)
    deriv_bf = loss_slope(
        rebuilt, values, loss_kind.reshape(tile_rows * tile_depth, tile_cols)
    ).astype(jnp.bfloat16)
    projected = jnp.dot(deriv_bf, half_two, preferred_element_type=jnp.float32).reshape(
        tile_rows, tile_depth, rank_width
    )
    grad_one = jnp.sum(projected * three_f[None, :, :], axis=1) * scales[0]
    grad_three = jnp.sum(projected * one_f[:, None, :], axis=0) * scales[2]
    grad_two = (
        lax.dot_general(
            deriv_bf, scaled_rows, (((0,), (0,)), ((), ())), preferred_element_type=jnp.float32
        )
        * scales[1]
    )
    return (grad_one, grad_two, grad_three)


def third_sum(grad_three):
    return lax.psum(grad_three, ("row", "col"))


def shards(
    tensor,
    loss_kind,
    factor_one,
    factor_two,
    factor_three,
    first_one,
    second_one,
    first_two,
    second_two,
    first_three,
    second_three,
):
    tile_rows, tile_depth, tile_cols = tensor.shape
    full_rows = tile_rows * lax.axis_size("row")
    full_cols = tile_cols * lax.axis_size("col")
    scales = (
        1.0 / math.sqrt(full_cols * tile_depth),
        1.0 / math.sqrt(full_rows * tile_depth),
        1.0 / math.sqrt(full_rows * full_cols),
    )
    start_one, start_two, start_three = (factor_one, factor_two, factor_three)
    for iteration in range(ITERS):
        half_one = lax.all_gather(factor_one.astype(jnp.bfloat16), "col", axis=0, tiled=True)
        half_two = lax.all_gather(factor_two.astype(jnp.bfloat16), "row", axis=0, tiled=True)
        grad_one, grad_two, grad_three = tile_grads(
            tensor, loss_kind, half_one, half_two, factor_three.astype(jnp.bfloat16), scales
        )
        grad_one = lax.psum_scatter(grad_one, "col", scatter_dimension=0, tiled=True)
        grad_two = lax.psum_scatter(grad_two, "row", scatter_dimension=0, tiled=True)
        grad_three = third_sum(grad_three)
        counter = STEP + iteration + 1
        factor_one, first_one, second_one = adam_step(
            factor_one, first_one, second_one, grad_one, counter
        )
        factor_two, first_two, second_two = adam_step(
            factor_two, first_two, second_two, grad_two, counter
        )
        factor_three, first_three, second_three = adam_step(
            factor_three, first_three, second_three, grad_three, counter
        )
    spread = learn_rate * ITERS
    return (
        (start_one - factor_one) / spread,
        (start_two - factor_two) / spread,
        (start_three - factor_three) / spread,
    )


def solution(mesh):
    in_specs = (
        P("row", None, "col"),
        P("row", None, "col"),
        P(("row", "col"), None),
        P(("col", "row"), None),
        P(),
        P(("row", "col"), None),
        P(("row", "col"), None),
        P(("col", "row"), None),
        P(("col", "row"), None),
        P(),
        P(),
    )
    out_specs = (P(("row", "col"), None), P(("col", "row"), None), P())
    return jax.shard_map(shards, mesh=mesh, in_specs=in_specs, out_specs=out_specs, check_vma=False)
```

profile of v0, /device:TPU:0, one launch (start us, length us, event | category | flops | bytes accessed | tf_op | source)
XLA Modules:
  0.0 399.3 jit_solution(8798334853152890748)
XLA Ops:
  8.0 0.0 all-reduce.3.cloned.1.call-start
  8.0 0.8 convert_element_type.63
  8.8 0.8 convert_element_type.57
  9.7 6.5 %all_gather.12 = bf16[128,512]{1,0:T(8,128)(2,1)S(1)} all-gather(bf16[32,512]{1,0:T(8,128)(2,1)S(1)} %convert_element_type.57), channel_id=1, replica_groups=mesh['row'=8,'col'=4] {'col'}, dimensions={0}, use_global_device_ids=true | all-gather | bytes 163840 | tf_op jit(solution)/shard_map/all_gather | solution.py:90
  16.1 31.3 %all_gather.13 = bf16[128,512]{1,0:T(8,128)(2,1)S(1)} all-gather(bf16[16,512]{1,0:T(8,128)(2,1)S(1)} %convert_element_type.63), channel_id=1, replica_groups=mesh['row'=8,'col'=4] {'row'}, dimensions={0}, use_global_device_ids=true | all-gather | bytes 147456 | tf_op jit(solution)/shard_map/all_gather | solution.py:91
  47.4 0.9 convert_convert_fusion
  48.3 2.8 broadcast_compare_fusion
  51.1 0.0 copy-start.3
  51.1 0.0 copy-start.17
  51.1 3.3 multiply_convert_fusion.1
  54.5 2.4 fusion.1
  56.9 0.8 copy-done.1
  57.7 8.1 %multiply_reduce_fusion.3 = (f32[128,512]{1,0:T(8,128)S(1)}, f32[8192,512]{1,0:T(8,128)}) fusion(f32[64,512]{1,0:T(8,128)S(1)} %convert_convert_fusion, bf16[8192,128]{1,0:T(8,128)(2,1)S(1)} %fusion.1, bf16[128,512]{1,0:T(8,128)(2,1)S(1)} %all_gather.13), kind=kOutput, calls=%fused_computation.4 | convolution fusion | flops 1082064896 | bytes 19398656 | tf_op jit(solution)/shard_map/dot_general | solution.py:49
  65.8 8.4 %multiply_reduce_fusion.2 = f32[64,512]{1,0:T(8,128)S(1)} fusion(f32[128,64,512]{2,1,0:T(8,128)} %bitcast.30, f32[128,512]{1,0:T(8,128)S(1)} %convert_element_type.58), kind=kLoop, calls=%fused_computation.3 | loop fusion | flops 8355840 | bytes 17170432 | tf_op jit(solution)/shard_map/reduce_sum | solution.py:53
  74.2 0.7 broadcast_multiply_fusion.3
  74.9 0.0 all-reduce.3.cloned.1.call-update
  74.9 0.0 copy-start.2
  74.9 0.0 copy-start.6
  74.9 0.0 copy-start.7
  74.9 0.0 copy-start.9
  75.0 0.0 copy-start.13
  75.0 0.0 copy-start.14
  75.0 0.0 copy-start.5
  75.0 0.0 copy-start.10
  75.0 0.0 copy-start.11
  75.0 0.0 reduce-scatter.7.cloned.1.call-start
  75.1 5.5 %convolution_multiply_fusion.1 = f32[128,512]{1,0:T(8,128)} fusion(bf16[8192,128]{1,0:T(8,128)(2,1)S(1)} %fusion.1, bf16[8192,512]{1,0:T(8,128)(2,1)} %bitcast.35), kind=kOutput, calls=%fused_computation.19 | convolution fusion | flops 1073807360 | bytes 10747904 | tf_op jit(solution)/shard_map/dot_general | solution.py:55
  80.6 0.0 reduce-scatter.7.cloned.1.call-update
  80.6 0.0 reduce-scatter.5.cloned.1.call-start
  80.7 0.7 broadcast_multiply_fusion.1
  81.4 0.0 reduce-scatter.5.cloned.1.call-update
  81.4 0.0 all-reduce.5.cloned.1.call-start
  81.5 119.0 %all-reduce.3.cloned.1.call-done = f32[64,512]{1,0:T(8,128)} async-done(((f32[64,512]{1,0:T(8,128)}), f32[64,512]{1,0:T(8,128)}) %all-reduce.3.cloned.1.call-update) | async-done | bytes 131088 | tf_op jit(solution)/shard_map/psum | solution.py:64
  200.5 0.0 copy-done.7
  200.5 1.0 fusion.24
  201.5 0.0 reduce-scatter.7.cloned.1.call-done
  201.6 0.8 fusion.36
  202.4 30.5 %all_gather.15 = bf16[128,512]{1,0:T(8,128)(2,1)S(1)} all-gather(bf16[16,512]{1,0:T(8,128)(2,1)S(1)} %fusion.36), channel_id=1, replica_groups=mesh['row'=8,'col'=4] {'row'}, dimensions={0}, use_global_device_ids=true | all-gather | bytes 147456 | tf_op jit(solution)/shard_map/all_gather | solution.py:91
  232.9 0.0 copy-done.11
  232.9 0.9 fusion.26
  233.8 5.6 %all_gather.14 = bf16[128,512]{1,0:T(8,128)(2,1)S(1)} all-gather(bf16[32,512]{1,0:T(8,128)(2,1)S(1)} %fusion.26), channel_id=1, replica_groups=mesh['row'=8,'col'=4] {'col'}, dimensions={0}, use_global_device_ids=true | all-gather | bytes 163840 | tf_op jit(solution)/shard_map/all_gather | solution.py:90
  239.4 0.0 copy-start.18
  239.4 3.3 multiply_convert_fusion
  242.8 2.4 fusion.3
  245.2 0.8 copy-done
  246.0 8.1 %multiply_reduce_fusion.1 = (f32[128,512]{1,0:T(8,128)S(1)}, f32[8192,512]{1,0:T(8,128)}) fusion(f32[64,512]{1,0:T(8,128)S(1)} %fusion.24, bf16[8192,128]{1,0:T(8,128)(2,1)S(1)} %fusion.3, bf16[128,512]{1,0:T(8,128)(2,1)S(1)} %all_gather.15), kind=kOutput, calls=%fused_computation.1 | convolution fusion | flops 1082064896 | bytes 19398656 | tf_op jit(solution)/shard_map/dot_general | solution.py:49
  254.1 8.4 %multiply_reduce_fusion = f32[64,512]{1,0:T(8,128)S(1)} fusion(f32[128,64,512]{2,1,0:T(8,128)} %bitcast.31, f32[128,512]{1,0:T(8,128)S(1)} %convert_element_type.68), kind=kLoop, calls=%fused_computation | loop fusion | flops 8355840 | bytes 17170432 | tf_op jit(solution)/shard_map/reduce_sum | solution.py:53
  262.5 0.7 broadcast_multiply_fusion.2
  263.2 0.0 all-reduce.5.cloned.1.call-update
  263.2 0.0 copy-start.8
  263.2 0.0 copy-start.15
  263.2 0.0 reduce-scatter.11.cloned.1.call-start
  263.3 5.4 %convolution_multiply_fusion = f32[128,512]{1,0:T(8,128)} fusion(bf16[8192,128]{1,0:T(8,128)(2,1)S(1)} %fusion.3, bf16[8192,512]{1,0:T(8,128)(2,1)} %bitcast.33), kind=kOutput, calls=%fused_computation.18 | convolution fusion | flops 1073807360 | bytes 10747904 | tf_op jit(solution)/shard_map/dot_general | solution.py:55
  268.7 0.0 reduce-scatter.11.cloned.1.call-update
  268.7 0.0 reduce-scatter.9.cloned.1.call-start
  268.8 0.7 broadcast_multiply_fusion
  269.5 0.0 reduce-scatter.9.cloned.1.call-update
  269.5 117.4 %all-reduce.5.cloned.1.call-done = f32[64,512]{1,0:T(8,128)} async-done(((f32[64,512]{1,0:T(8,128)}), f32[64,512]{1,0:T(8,128)}) %all-reduce.5.cloned.1.call-update) | async-done | bytes 131088 | tf_op jit(solution)/shard_map/psum | solution.py:64
  386.9 0.0 copy-done.8
  386.9 1.7 fusion.14
  388.7 0.0 copy-done.15
  388.7 1.4 fusion.35
  390.1 0.0 copy-done.12
  390.1 1.6 fusion.25
  (22 shorter events, 0.1 us)
Async XLA Ops:
  8.0 192.5 %all-reduce.3.cloned.1.call-start = ((), (), s32[]{:S(2)}) async-start(), calls=%async_computation.5 | async-start | bytes 262144 | tf_op jit(solution)/shard_map/psum | solution.py:64
  51.1 3.4 copy-start.3
  51.1 3.4 copy-start.17
  54.5 3.2 copy-start.1
  74.9 125.6 %copy-start.2 = (f32[64,512]{1,0:T(8,128)S(1)}, f32[64,512]{1,0:T(8,128)}, u32[]{:S(2)}) copy-start(f32[64,512]{1,0:T(8,128)} %param.15) | copy-start | bytes 393220
  74.9 125.6 %copy-start.6 = (f32[64,512]{1,0:T(8,128)S(1)}, f32[64,512]{1,0:T(8,128)}, u32[]{:S(2)}) copy-start(f32[64,512]{1,0:T(8,128)} %param.20) | copy-start | bytes 393220
  74.9 125.6 %copy-start.7 = (f32[64,512]{1,0:T(8,128)S(1)}, f32[64,512]{1,0:T(8,128)}, u32[]{:S(2)}) copy-start(f32[64,512]{1,0:T(8,128)} %param.21) | copy-start | bytes 393220
  74.9 126.6 %copy-start.9 = (f32[16,512]{1,0:T(8,128)S(1)}, f32[16,512]{1,0:T(8,128)}, u32[]{:S(2)}) copy-start(f32[16,512]{1,0:T(8,128)} %param.14) | copy-start | bytes 98308
  75.0 126.6 %copy-start.13 = (f32[16,512]{1,0:T(8,128)S(1)}, f32[16,512]{1,0:T(8,128)}, u32[]{:S(2)}) copy-start(f32[16,512]{1,0:T(8,128)} %param.18) | copy-start | bytes 98308
  75.0 126.6 %copy-start.14 = (f32[16,512]{1,0:T(8,128)S(1)}, f32[16,512]{1,0:T(8,128)}, u32[]{:S(2)}) copy-start(f32[16,512]{1,0:T(8,128)} %param.19) | copy-start | bytes 98308
  75.0 157.9 %copy-start.5 = (f32[32,512]{1,0:T(8,128)S(1)}, f32[32,512]{1,0:T(8,128)}, u32[]{:S(2)}) copy-start(f32[32,512]{1,0:T(8,128)} %param.13) | copy-start | bytes 196612
  75.0 157.9 %copy-start.10 = (f32[32,512]{1,0:T(8,128)S(1)}, f32[32,512]{1,0:T(8,128)}, u32[]{:S(2)}) copy-start(f32[32,512]{1,0:T(8,128)} %param.16) | copy-start | bytes 196612
  75.0 157.9 %copy-start.11 = (f32[32,512]{1,0:T(8,128)S(1)}, f32[32,512]{1,0:T(8,128)}, u32[]{:S(2)}) copy-start(f32[32,512]{1,0:T(8,128)} %param.17) | copy-start | bytes 196612
  75.0 126.5 %reduce-scatter.7.cloned.1.call-start = ((), (), s32[]{:S(2)}) async-start(), calls=%async_computation.6 | async-start | bytes 294912 | tf_op jit(solution)/shard_map/reduce_scatter | solution.py:96
  80.6 152.3 %reduce-scatter.5.cloned.1.call-start = ((), (), s32[]{:S(2)}) async-start(), calls=%async_computation.4 | async-start | bytes 327680 | tf_op jit(solution)/shard_map/reduce_scatter | solution.py:95
  81.4 305.5 %all-reduce.5.cloned.1.call-start = ((), (), s32[]{:S(2)}) async-start(), calls=%async_computation.9 | async-start | bytes 262144 | tf_op jit(solution)/shard_map/psum | solution.py:64
  239.4 3.4 copy-start.4
  239.4 3.4 copy-start.18
  242.8 3.2 copy-start
  263.2 123.7 %copy-start.8 = (f32[64,512]{1,0:T(8,128)S(1)}, f32[64,512]{1,0:T(8,128)}, u32[]{:S(2)}) copy-start(f32[64,512]{1,0:T(8,128)} %all-reduce.3.cloned.1.call-done) | copy-start | bytes 393220
  263.2 125.5 %copy-start.15 = (f32[16,512]{1,0:T(8,128)S(1)}, f32[16,512]{1,0:T(8,128)}, u32[]{:S(2)}) copy-start(f32[16,512]{1,0:T(8,128)} %param.19) | copy-start | bytes 98308
  263.2 125.5 %copy-start.16 = (f32[16,512]{1,0:T(8,128)S(1)}, f32[16,512]{1,0:T(8,128)}, u32[]{:S(2)}) copy-start(f32[16,512]{1,0:T(8,128)} %reduce-scatter.7.cloned.1.call-done) | copy-start | bytes 98308
  263.2 126.9 %copy-start.12 = (f32[32,512]{1,0:T(8,128)S(1)}, f32[32,512]{1,0:T(8,128)}, u32[]{:S(2)}) copy-start(f32[32,512]{1,0:T(8,128)} %reduce-scatter.5.cloned.1.call-done) | copy-start | bytes 196612
  263.2 125.4 %reduce-scatter.11.cloned.1.call-start = ((), (), s32[]{:S(2)}) async-start(), calls=%async_computation.8 | async-start | bytes 294912 | tf_op jit(solution)/shard_map/reduce_scatter | solution.py:96
  268.7 121.4 %reduce-scatter.9.cloned.1.call-start = ((), (), s32[]{:S(2)}) async-start(), calls=%async_computation.7 | async-start | bytes 327680 | tf_op jit(solution)/shard_map/reduce_scatter | solution.py:95
Sparse Core Ops, SparseCore 0:
  75.0 125.4 all-reduce.2
  263.3 123.5 all-reduce.4
Sparse Core Ops, SparseCore 1:
  80.7 63.0 reduce-scatter.6
  146.1 19.0 reduce-scatter.4
  268.8 61.1 reduce-scatter.10
  332.5 19.0 reduce-scatter.8
where the time goes:
time: 400 us; the launch traced here: 399 us
  waiting for transfers between devices  237 us (59%)
  blocking collectives  73.9 us (18%)
  other arithmetic  39.1 us (10%)
  matrix products  31.8 us (8%)
  between operations  16 us (4%)
    psum x2, waiting for transfers between devices, third_sum(): return lax.psum(grad_three, ('row', 'col'))  236 us
    all_gather x2, blocking collectives, shards(): lax.all_gather(factor_two.astype(jnp.bfloat16), 'row', axis=0, tiled=True)  61.8 us
    reduce_sum x2, other arithmetic, tile_grads(): grad_three = jnp.sum(projected * one_f[:, None, :], axis=0) * scales[2]  16.8 us
    dot_general x2, matrix products, tile_grads(): jnp.dot(deriv_bf, half_two, preferred_element_type=jnp.float32)  16.2 us
    all_gather x2, blocking collectives, shards(): lax.all_gather(factor_one.astype(jnp.bfloat16), 'col', axis=0, tiled=True)  12.1 us
    dot_general x2, matrix products, tile_grads(): lax.dot_general(deriv_bf, scaled_rows, (((0,), (0,)), ((), ())), preferre...  10.9 us
  transfers between devices with their start and end apart: 6, of which 2 were waited for; matrix products, arithmetic and copies ran while one was open for 4% of the time, Pallas kernels for 0%

commit v1 on v0

--- a/solution.py
+++ b/solution.py
@@ -61,7 +61,7 @@
 
 
 def third_sum(grad_three):
-    return lax.psum(grad_three, ("row", "col"))
+    return jnp.sum(lax.all_gather(grad_three, ("row", "col")), axis=0)
 
 
 def shards(

time: 400 us -> 297 us (0.74)
  waiting for transfers between devices: 237 us -> 135 us
    psum x2 -> x0, waiting for transfers between devices: 236 us -> none  [third_sum(): return lax.psum(grad_three, ('row', 'col'))]
    reduce_scatter x2, waiting for transfers between devices: 0.03 us -> 108 us  [shards(): lax.psum_scatter(grad_two, 'row', scatter_dimension=0, tiled=True)]
    reduce_scatter x2, waiting for transfers between devices: 0.01 us -> 25.9 us  [shards(): lax.psum_scatter(grad_one, 'col', scatter_dimension=0, tiled=True)]
    reduce_sum x0 -> x2, other arithmetic: none -> 5.06 us  [third_sum(): return jnp.sum(lax.all_gather(grad_three, ('row', 'col')), axis=0)]
  transfers between devices with their start and end apart: 6 -> 6, of which waited for: 2 -> 4; matrix products, arithmetic and copies ran while one was open for 4% -> 13% of each run, Pallas kernels for 0% -> 0%
where the time goes in v1:
time: 297 us; the launch traced here: 296 us
  waiting for transfers between devices  135 us (45%)
  blocking collectives  73.8 us (25%)
  other arithmetic  42.6 us (14%)
  matrix products  28.3 us (10%)
  between operations  15.5 us (5%)
    reduce_scatter x2, waiting for transfers between devices, shards(): lax.psum_scatter(grad_two, 'row', scatter_dimension=0, tiled=True)  108 us
    all_gather x2, blocking collectives, shards(): lax.all_gather(factor_two.astype(jnp.bfloat16), 'row', axis=0, tiled=True)  61.9 us
    reduce_scatter x2, waiting for transfers between devices, shards(): lax.psum_scatter(grad_one, 'col', scatter_dimension=0, tiled=True)  25.9 us
    reduce_sum x2, other arithmetic, tile_grads(): grad_three = jnp.sum(projected * one_f[:, None, :], axis=0) * scales[2]  17.1 us
    dot_general x2, matrix products, tile_grads(): jnp.dot(deriv_bf, half_two, preferred_element_type=jnp.float32)  16.2 us
    all_gather x2, blocking collectives, shards(): lax.all_gather(factor_one.astype(jnp.bfloat16), 'col', axis=0, tiled=True)  11.9 us
    dot_general x2, matrix products, tile_grads(): lax.dot_general(deriv_bf, scaled_rows, (((0,), (0,)), ((), ())), preferre...  7.37 us
    convert_element_type x2, other arithmetic, tile_grads(): scaled_rows = (one_f[:, None, :] * three_f[None, :, :]).astype(jnp.bfloat...  6.65 us
  transfers between devices with their start and end apart: 6, of which 4 were waited for; matrix products, arithmetic and copies ran while one was open for 13% of the time, Pallas kernels for 0%

profile of v1, /device:TPU:0, one launch (start us, length us, event | category | flops | bytes accessed | tf_op | source)
XLA Modules:
  0.0 296.2 jit_solution(6067091528592303479)
XLA Ops:
  8.0 0.0 reduce-scatter.5.cloned.1.call-start
  8.0 0.8 convert_element_type.63
  8.8 0.8 convert_element_type.57
  9.7 6.5 %all_gather.20 = bf16[128,512]{1,0:T(8,128)(2,1)S(1)} all-gather(bf16[32,512]{1,0:T(8,128)(2,1)S(1)} %convert_element_type.57), channel_id=1, replica_groups=mesh['row'=8,'col'=4] {'col'}, dimensions={0}, use_global_device_ids=true | all-gather | bytes 163840 | tf_op jit(solution)/shard_map/all_gather | solution.py:90
  16.1 31.3 %all_gather.21 = bf16[128,512]{1,0:T(8,128)(2,1)S(1)} all-gather(bf16[16,512]{1,0:T(8,128)(2,1)S(1)} %convert_element_type.63), channel_id=1, replica_groups=mesh['row'=8,'col'=4] {'row'}, dimensions={0}, use_global_device_ids=true | all-gather | bytes 147456 | tf_op jit(solution)/shard_map/all_gather | solution.py:91
  47.4 0.9 convert_convert_fusion
  48.3 2.8 broadcast_compare_fusion
  51.1 0.0 copy-start.2
  51.1 0.0 copy-start.14
  51.2 3.3 %multiply_convert_fusion.1 = bf16[128,64,512]{2,1,0:T(8,128)(2,1)S(1)} fusion(f32[64,512]{1,0:T(8,128)S(1)} %convert_convert_fusion, f32[128,512]{1,0:T(8,128)S(1)} %convert_element_type.58), kind=kLoop, calls=%fused_computation.5 | loop fusion | flops 8388608 | bytes 8781824 | tf_op jit(solution)/shard_map/convert_element_type | solution.py:39
  54.5 0.0 copy-start
  54.5 0.0 copy-done.2
  54.5 0.0 copy-done.14
  54.5 2.4 fusion.1
  56.9 0.8 copy-done
  57.7 8.1 %multiply_reduce_fusion.3 = (f32[128,512]{1,0:T(8,128)S(1)}, f32[8192,512]{1,0:T(8,128)}) fusion(f32[64,512]{1,0:T(8,128)S(1)} %convert_convert_fusion, bf16[8192,128]{1,0:T(8,128)(2,1)S(1)} %fusion.1, bf16[128,512]{1,0:T(8,128)(2,1)S(1)} %all_gather.21), kind=kOutput, calls=%fused_computation.4 | convolution fusion | flops 1082064896 | bytes 19398656 | tf_op jit(solution)/shard_map/dot_general | solution.py:49
  65.8 0.7 broadcast_multiply_fusion.1
  66.5 0.0 reduce-scatter.5.cloned.1.call-update
  66.5 0.0 reduce-scatter.7.cloned.1.call-start
  66.6 5.4 %convolution_multiply_fusion.1 = f32[128,512]{1,0:T(8,128)} fusion(bf16[8192,128]{1,0:T(8,128)(2,1)S(1)} %fusion.1, bf16[8192,512]{1,0:T(8,128)(2,1)} %bitcast.35), kind=kOutput, calls=%fused_computation.19 | convolution fusion | flops 1073807360 | bytes 10747904 | tf_op jit(solution)/shard_map/dot_general | solution.py:55
  72.0 0.0 reduce-scatter.7.cloned.1.call-update
  72.0 0.2 all-gather.5.cloned.1.call-start
  72.2 0.0 copy-start.4
  72.2 0.0 copy-start.8
  72.2 0.0 copy-start.9
  72.2 0.0 copy-start.7
  72.3 0.0 copy-start.11
  72.3 0.0 copy-start.12
  72.3 8.6 %multiply_reduce_fusion.2 = f32[64,512]{1,0:T(8,128)S(1)} fusion(f32[128,64,512]{2,1,0:T(8,128)} %bitcast.32, f32[128,512]{1,0:T(8,128)S(1)} %convert_element_type.58), kind=kLoop, calls=%fused_computation.3 | loop fusion | flops 8355840 | bytes 17170432 | tf_op jit(solution)/shard_map/reduce_sum | solution.py:53
  80.9 0.0 copy-start.5
  80.9 0.0 copy-start.6
  80.9 0.7 broadcast_multiply_fusion.3
  81.6 0.0 all-gather.5.cloned.1.call-update
  81.6 0.0 reduce-scatter.11.cloned.1.call-start
  81.7 5.9 %reduce-scatter.5.cloned.1.call-done = f32[32,512]{1,0:T(8,128)} async-done(((f32[128,512]{1,0:T(8,128)}), f32[32,512]{1,0:T(8,128)}) %reduce-scatter.5.cloned.1.call-update) | async-done | bytes 65552 | tf_op jit(solution)/shard_map/reduce_scatter | solution.py:95
  87.6 0.9 fusion.26
  88.5 5.4 %all_gather.22 = bf16[128,512]{1,0:T(8,128)(2,1)S(1)} all-gather(bf16[32,512]{1,0:T(8,128)(2,1)S(1)} %fusion.26), channel_id=1, replica_groups=mesh['row'=8,'col'=4] {'col'}, dimensions={0}, use_global_device_ids=true | all-gather | bytes 163840 | tf_op jit(solution)/shard_map/all_gather | solution.py:90
  94.0 65.5 %reduce-scatter.7.cloned.1.call-done = f32[16,512]{1,0:T(8,128)} async-done(((f32[128,512]{1,0:T(8,128)}), f32[16,512]{1,0:T(8,128)}) %reduce-scatter.7.cloned.1.call-update) | async-done | bytes 32784 | tf_op jit(solution)/shard_map/reduce_scatter | solution.py:96
  159.4 0.0 copy-done.12
  159.4 0.8 fusion.36
  160.2 30.6 %all_gather.24 = bf16[128,512]{1,0:T(8,128)(2,1)S(1)} all-gather(bf16[16,512]{1,0:T(8,128)(2,1)S(1)} %fusion.36), channel_id=1, replica_groups=mesh['row'=8,'col'=4] {'row'}, dimensions={0}, use_global_device_ids=true | all-gather | bytes 147456 | tf_op jit(solution)/shard_map/all_gather | solution.py:91
  190.8 2.5 reduce_sum.56
  193.4 0.1 fusion.24
  193.5 0.0 copy-start.15
  193.5 3.3 %multiply_convert_fusion = bf16[128,64,512]{2,1,0:T(8,128)(2,1)S(1)} fusion(f32[64,512]{1,0:T(8,128)S(1)} %fusion.24, f32[128,512]{1,0:T(8,128)S(1)} %convert_element_type.68), kind=kLoop, calls=%fused_computation.2 | loop fusion | flops 8388608 | bytes 8781824 | tf_op jit(solution)/shard_map/convert_element_type | solution.py:39
  196.9 2.4 fusion.3
  199.2 2.0 convolution_multiply_fusion
  201.2 0.0 reduce-scatter.11.cloned.1.call-update
  201.3 0.3 reduce-scatter.9.cloned.1.call-start
  201.5 8.1 %multiply_reduce_fusion.1 = (f32[128,512]{1,0:T(8,128)S(1)}, f32[8192,512]{1,0:T(8,128)}) fusion(f32[64,512]{1,0:T(8,128)S(1)} %fusion.24, bf16[8192,128]{1,0:T(8,128)(2,1)S(1)} %fusion.3, bf16[128,512]{1,0:T(8,128)(2,1)S(1)} %all_gather.24), kind=kOutput, calls=%fused_computation.1 | convolution fusion | flops 1082064896 | bytes 19398656 | tf_op jit(solution)/shard_map/dot_general | solution.py:49
  209.6 0.7 broadcast_multiply_fusion
  210.4 0.0 reduce-scatter.9.cloned.1.call-update
  210.4 0.0 all-gather.7.cloned.1.call-start
  210.4 0.0 copy-start.13
  210.4 0.0 copy-start.10
  210.5 8.5 %multiply_reduce_fusion = f32[64,512]{1,0:T(8,128)S(1)} fusion(f32[128,64,512]{2,1,0:T(8,128)} %bitcast.33, f32[128,512]{1,0:T(8,128)S(1)} %convert_element_type.68), kind=kLoop, calls=%fused_computation | loop fusion | flops 8355840 | bytes 17170432 | tf_op jit(solution)/shard_map/reduce_sum | solution.py:53
  219.0 0.7 broadcast_multiply_fusion.2
  219.6 0.0 all-gather.7.cloned.1.call-update
  219.7 43.0 %reduce-scatter.11.cloned.1.call-done = f32[16,512]{1,0:T(8,128)} async-done(((f32[128,512]{1,0:T(8,128)}), f32[16,512]{1,0:T(8,128)}) %reduce-scatter.11.cloned.1.call-update) | async-done | bytes 32784 | tf_op jit(solution)/shard_map/reduce_scatter | solution.py:96
  262.7 1.4 fusion.35
  264.1 20.0 %reduce-scatter.9.cloned.1.call-done = f32[32,512]{1,0:T(8,128)} async-done(((f32[128,512]{1,0:T(8,128)}), f32[32,512]{1,0:T(8,128)}) %reduce-scatter.9.cloned.1.call-update) | async-done | bytes 65552 | tf_op jit(solution)/shard_map/reduce_scatter | solution.py:95
  284.1 1.6 fusion.25
  285.7 2.5 reduce_sum.59
  288.2 0.8 fusion.14
  (18 shorter events, 0.1 us)
Async XLA Ops:
  8.0 79.6 %reduce-scatter.5.cloned.1.call-start = ((), (), s32[]{:S(2)}) async-start(), calls=%async_computation.4 | async-start | bytes 327680 | tf_op jit(solution)/shard_map/reduce_scatter | solution.py:95
  51.1 3.4 %copy-start.2 = (pred[128,64,128]{2,1,0:T(32,128)(4,1)}, pred[128,64,128]{2,1,0:T(32,128)(4,1)S(1)}, u32[]{:S(2)}) copy-start(pred[128,64,128]{2,1,0:T(32,128)(4,1)S(1)} %broadcast_compare_fusion) | copy-start | bytes 3145732
  51.1 3.4 %copy-start.14 = (bf16[128,64,128]{2,1,0:T(8,128)(2,1)S(1)}, bf16[128,64,128]{2,1,0:T(8,128)(2,1)}, u32[]{:S(2)}) copy-start(bf16[128,64,128]{2,1,0:T(8,128)(2,1)} %param.11) | copy-start | bytes 6291460
  54.5 3.2 %copy-start = (bf16[128,64,512]{2,1,0:T(8,128)(2,1)}, bf16[128,64,512]{2,1,0:T(8,128)(2,1)S(1)}, u32[]{:S(2)}) copy-start(bf16[128,64,512]{2,1,0:T(8,128)(2,1)S(1)} %multiply_convert_fusion.1) | copy-start | bytes 25165828
  66.5 92.9 %reduce-scatter.7.cloned.1.call-start = ((), (), s32[]{:S(2)}) async-start(), calls=%async_computation.5 | async-start | bytes 294912 | tf_op jit(solution)/shard_map/reduce_scatter | solution.py:96
  72.0 118.8 %all-gather.5.cloned.1.call-start = ((), (), s32[]{:S(2)}) async-start(), calls=%async_computation.8 | async-start | bytes 4325376 | tf_op jit(solution)/shard_map/all_gather | solution.py:64
  72.2 15.4 %copy-start.4 = (f32[32,512]{1,0:T(8,128)S(1)}, f32[32,512]{1,0:T(8,128)}, u32[]{:S(2)}) copy-start(f32[32,512]{1,0:T(8,128)} %param.13) | copy-start | bytes 196612
  72.2 15.4 %copy-start.8 = (f32[32,512]{1,0:T(8,128)S(1)}, f32[32,512]{1,0:T(8,128)}, u32[]{:S(2)}) copy-start(f32[32,512]{1,0:T(8,128)} %param.16) | copy-start | bytes 196612
  72.2 15.4 %copy-start.9 = (f32[32,512]{1,0:T(8,128)S(1)}, f32[32,512]{1,0:T(8,128)}, u32[]{:S(2)}) copy-start(f32[32,512]{1,0:T(8,128)} %param.17) | copy-start | bytes 196612
  72.2 87.2 %copy-start.7 = (f32[16,512]{1,0:T(8,128)S(1)}, f32[16,512]{1,0:T(8,128)}, u32[]{:S(2)}) copy-start(f32[16,512]{1,0:T(8,128)} %param.14) | copy-start | bytes 98308
  72.3 87.2 %copy-start.11 = (f32[16,512]{1,0:T(8,128)S(1)}, f32[16,512]{1,0:T(8,128)}, u32[]{:S(2)}) copy-start(f32[16,512]{1,0:T(8,128)} %param.18) | copy-start | bytes 98308
  72.3 87.2 %copy-start.12 = (f32[16,512]{1,0:T(8,128)S(1)}, f32[16,512]{1,0:T(8,128)}, u32[]{:S(2)}) copy-start(f32[16,512]{1,0:T(8,128)} %param.19) | copy-start | bytes 98308
  80.9 112.5 %copy-start.1 = (f32[64,512]{1,0:T(8,128)S(1)}, f32[64,512]{1,0:T(8,128)}, u32[]{:S(2)}) copy-start(f32[64,512]{1,0:T(8,128)} %param.15) | copy-start | bytes 393220
  80.9 112.5 %copy-start.5 = (f32[64,512]{1,0:T(8,128)S(1)}, f32[64,512]{1,0:T(8,128)}, u32[]{:S(2)}) copy-start(f32[64,512]{1,0:T(8,128)} %param.20) | copy-start | bytes 393220
  80.9 112.5 %copy-start.6 = (f32[64,512]{1,0:T(8,128)S(1)}, f32[64,512]{1,0:T(8,128)}, u32[]{:S(2)}) copy-start(f32[64,512]{1,0:T(8,128)} %param.21) | copy-start | bytes 393220
  81.6 181.0 %reduce-scatter.11.cloned.1.call-start = ((), (), s32[]{:S(2)}) async-start(), calls=%async_computation.7 | async-start | bytes 294912 | tf_op jit(solution)/shard_map/reduce_scatter | solution.py:96
  193.5 3.4 %copy-start.3 = (pred[128,64,128]{2,1,0:T(32,128)(4,1)S(1)}, pred[128,64,128]{2,1,0:T(32,128)(4,1)}, u32[]{:S(2)}) copy-start(pred[128,64,128]{2,1,0:T(32,128)(4,1)} %copy-done.2) | copy-start | bytes 3145732
  193.5 3.4 %copy-start.15 = (bf16[128,64,128]{2,1,0:T(8,128)(2,1)S(1)}, bf16[128,64,128]{2,1,0:T(8,128)(2,1)}, u32[]{:S(2)}) copy-start(bf16[128,64,128]{2,1,0:T(8,128)(2,1)} %param.11) | copy-start | bytes 6291460
  201.3 82.8 %reduce-scatter.9.cloned.1.call-start = ((), (), s32[]{:S(2)}) async-start(), calls=%async_computation.6 | async-start | bytes 327680 | tf_op jit(solution)/shard_map/reduce_scatter | solution.py:95
  210.4 75.3 %all-gather.7.cloned.1.call-start = ((), (), s32[]{:S(2)}) async-start(), calls=%async_computation.9 | async-start | bytes 4325376 | tf_op jit(solution)/shard_map/all_gather | solution.py:64
  210.4 52.2 %copy-start.13 = (f32[16,512]{1,0:T(8,128)S(1)}, f32[16,512]{1,0:T(8,128)}, u32[]{:S(2)}) copy-start(f32[16,512]{1,0:T(8,128)} %reduce-scatter.7.cloned.1.call-done) | copy-start | bytes 98308
  210.4 73.7 %copy-start.10 = (f32[32,512]{1,0:T(8,128)S(1)}, f32[32,512]{1,0:T(8,128)}, u32[]{:S(2)}) copy-start(f32[32,512]{1,0:T(8,128)} %reduce-scatter.5.cloned.1.call-done) | copy-start | bytes 196612
Sparse Core Ops, SparseCore 0:
  66.7 20.9 reduce-scatter.4
  90.9 68.4 reduce-scatter.6
  201.4 61.2 reduce-scatter.10
  265.0 19.0 reduce-scatter.8
Sparse Core Ops, SparseCore 1:
  81.7 62.6 all-gather.4
  219.7 60.6 all-gather.6
